TPU v7x, 32 devices: a whole 2x2x4 slice. The times are simulated.
32 devices in a mesh: seq: 16 (over z, x, core), batch: 2 (over y).
Axes of the slice: x: 2, y: 2, z: 4, core: 2. Of those that a mesh axis runs over, the one named last changes fastest.
Arguments:
- inputs: bfloat16 [2, 4096, 1024], P('batch', 'seq'), may hold values from -6 to 6
- grad_out: bfloat16 [2, 4096, 1024], P('batch', 'seq'), may hold values from -6 to 6
- spectrum: float32 [2, 32, 256, 1024], P(None, 'seq', None, 'batch'), may hold values from -6 to 6
- first_moment: float32 [2, 32, 256, 1024], P(None, 'seq', None, 'batch'), may hold values from -2 to 2
- second_moment: float32 [2, 32, 256, 1024], P(None, 'seq', None, 'batch'), may hold values from 0.1 to 4
Outputs:
- new_spectrum: float32 [2, 32, 256, 1024], P(None, 'seq', None, 'batch')
- new_first: float32 [2, 32, 256, 1024], P(None, 'seq', None, 'batch')
- new_second: float32 [2, 32, 256, 1024], P(None, 'seq', None, 'batch')
- filtered: bfloat16 [2, 4096, 1024], P('batch', 'seq')
All inputs are finite; a program needn't handle non-finite values.
Results may differ from a plain program's by a relative error of at most 0.0055.
Values may be sent and summed in bfloat16 or wider, within the bound.
No kernel may reach another device: no remote copies, remote signals or barrier semaphores. Data moves between devices by JAX's collectives and lax.ppermute only.
A program may use at most 64 MiB of HBM per device.

v0:
```python
import math
import jax
import jax.numpy as jnp
from jax import lax
from jax.sharding import PartitionSpec as P

full_turn = 2.0 * math.pi
step_rate = 0.5
epsilon = 1e-06


def angles(numer, modulus):
    return full_turn * (numer % modulus).astype(jnp.float32) / modulus


def phase_pair(first_count, second_count, modulus):
    first_index = jnp.arange(first_count, dtype=jnp.int32)
    second_index = jnp.arange(second_count, dtype=jnp.int32)
    phases = angles(first_index[:, None] * second_index[None, :], modulus)
    return (jnp.cos(phases), jnp.sin(phases))


def local_forward(sequence, seq_count, point_count):
    batch_rows = sequence.shape[0]
    outer_count = 2 * seq_count
    full_length = outer_count * point_count
    values = sequence.reshape(batch_rows, seq_count, point_count, -1).astype(jnp.float32)
    outer_cos, outer_sin = phase_pair(outer_count, seq_count, outer_count)
    real_one = jnp.einsum("ja,bach->bjch", outer_cos, values, precision=lax.Precision.HIGHEST)
    imag_one = -jnp.einsum("ja,bach->bjch", outer_sin, values, precision=lax.Precision.HIGHEST)
    twist_cos, twist_sin = phase_pair(outer_count, point_count, full_length)
    twist_cos = twist_cos[None, :, :, None]
    twist_sin = twist_sin[None, :, :, None]
    real_two = real_one * twist_cos + imag_one * twist_sin
    imag_two = imag_one * twist_cos - real_one * twist_sin
    inner_cos, inner_sin = phase_pair(point_count, point_count, point_count)
    real_out = jnp.einsum(
        "cm,bjch->bjmh", inner_cos, real_two, precision=lax.Precision.HIGHEST
    ) + jnp.einsum("cm,bjch->bjmh", inner_sin, imag_two, precision=lax.Precision.HIGHEST)
    imag_out = jnp.einsum(
        "cm,bjch->bjmh", inner_cos, imag_two, precision=lax.Precision.HIGHEST
    ) - jnp.einsum("cm,bjch->bjmh", inner_sin, real_two, precision=lax.Precision.HIGHEST)
    return (real_out, imag_out)


def local_inverse(real_in, imag_in, seq_count, point_count):
    outer_count = 2 * seq_count
    full_length = outer_count * point_count
    inner_cos, inner_sin = phase_pair(point_count, point_count, point_count)
    real_one = jnp.einsum(
        "mc,bjmh->bjch", inner_cos, real_in, precision=lax.Precision.HIGHEST
    ) - jnp.einsum("mc,bjmh->bjch", inner_sin, imag_in, precision=lax.Precision.HIGHEST)
    imag_one = jnp.einsum(
        "mc,bjmh->bjch", inner_sin, real_in, precision=lax.Precision.HIGHEST
    ) + jnp.einsum("mc,bjmh->bjch", inner_cos, imag_in, precision=lax.Precision.HIGHEST)
    twist_cos, twist_sin = phase_pair(outer_count, point_count, full_length)
    twist_cos = twist_cos[None, :, :, None]
    twist_sin = twist_sin[None, :, :, None]
    real_two = real_one * twist_cos - imag_one * twist_sin
    imag_two = real_one * twist_sin + imag_one * twist_cos
    outer_cos, outer_sin = phase_pair(outer_count, seq_count, outer_count)
    result = jnp.einsum(
        "ja,bjch->bach", outer_cos, real_two, precision=lax.Precision.HIGHEST
    ) - jnp.einsum("ja,bjch->bach", outer_sin, imag_two, precision=lax.Precision.HIGHEST)
    return result / full_length


def channel_layout(inputs, grad_out, spectrum, first_moment, second_moment):
    seq_count = lax.axis_size("seq")
    batch_count = lax.axis_size("batch")
    batch_rows, point_count, channels = inputs.shape
    narrow = channels // (seq_count * batch_count)
    group_width = batch_count * narrow
    outer_count = 2 * seq_count
    full_length = outer_count * point_count
    local_outer = spectrum.shape[1]
    signal_parts = inputs.reshape(batch_rows, point_count, batch_count, seq_count, narrow)
    cotangent_parts = grad_out.reshape(batch_rows, point_count, batch_count, seq_count, narrow)
    signal_cols, cotangent_cols = (
        lax.all_to_all(signal_parts, "seq", split_axis=3, concat_axis=1, tiled=True),
        lax.all_to_all(cotangent_parts, "seq", split_axis=3, concat_axis=1, tiled=True),
    )
    state_shape = (2, local_outer, point_count, seq_count, narrow)
    spec_cols, first_cols, second_cols = (
        lax.all_to_all(
            spectrum.reshape(state_shape), "seq", split_axis=3, concat_axis=1, tiled=True
        ),
        lax.all_to_all(
            first_moment.reshape(state_shape), "seq", split_axis=3, concat_axis=1, tiled=True
        ),
        lax.all_to_all(
            second_moment.reshape(state_shape), "seq", split_axis=3, concat_axis=1, tiled=True
        ),
    )
    own_shape = (2, outer_count, point_count, narrow)
    spec_cols = spec_cols.reshape(own_shape)
    first_cols = first_cols.reshape(own_shape)
    second_cols = second_cols.reshape(own_shape)
    signal_real, signal_imag = local_forward(
        signal_cols.reshape(batch_rows, seq_count * point_count, group_width),
        seq_count,
        point_count,
    )
    cotangent_real, cotangent_imag = local_forward(
        cotangent_cols.reshape(batch_rows, seq_count * point_count, group_width),
        seq_count,
        point_count,
    )
    real_term = jnp.sum(signal_real * cotangent_real + signal_imag * cotangent_imag, axis=0)
    imag_term = jnp.sum(signal_real * cotangent_imag - signal_imag * cotangent_real, axis=0)
    local_grad = (jnp.stack([real_term, imag_term]) / full_length).reshape(
        2, outer_count, point_count, batch_count, narrow
    )
    own_grad = (
        lax.psum_scatter(local_grad.astype(jnp.bfloat16), "batch", scatter_dimension=3, tiled=True)
        .astype(jnp.float32)
        .reshape(own_shape)
    )
    new_first = 0.9 * first_cols + 0.1 * own_grad
    new_second = 0.99 * second_cols + 0.01 * own_grad * own_grad
    new_spectrum = spec_cols - step_rate * jnp.tanh(new_first / (jnp.sqrt(new_second) + epsilon))
    group_filter = lax.all_gather(new_spectrum, "batch", axis=3, tiled=True)
    filter_real = group_filter[0][None]
    filter_imag = group_filter[1][None]
    mixed_real = signal_real * filter_real - signal_imag * filter_imag
    mixed_imag = signal_real * filter_imag + signal_imag * filter_real
    rows_back = local_inverse(mixed_real, mixed_imag, seq_count, point_count)
    rows_back = rows_back.astype(jnp.bfloat16).reshape(
        batch_rows, seq_count * point_count, batch_count, 1, narrow
    )
    back_shape = (2, outer_count, point_count, 1, narrow)
    spec_back, first_back, second_back = (
        lax.all_to_all(
            new_spectrum.reshape(back_shape), "seq", split_axis=1, concat_axis=3, tiled=True
        ),
        lax.all_to_all(
            new_first.reshape(back_shape), "seq", split_axis=1, concat_axis=3, tiled=True
        ),
        lax.all_to_all(
            new_second.reshape(back_shape), "seq", split_axis=1, concat_axis=3, tiled=True
        ),
    )
    filtered = lax.all_to_all(rows_back, "seq", split_axis=1, concat_axis=3, tiled=True)
    final_shape = spectrum.shape
    return (
        spec_back.reshape(final_shape),
        first_back.reshape(final_shape),
        second_back.reshape(final_shape),
        filtered.reshape(batch_rows, point_count, channels),
    )


def per_device(inputs, grad_out, spectrum, first_moment, second_moment):
    return channel_layout(inputs, grad_out, spectrum, first_moment, second_moment)


def solution(mesh):
    return jax.shard_map(
        per_device,
        mesh=mesh,
        in_specs=(
            P("batch", "seq", None),
            P("batch", "seq", None),
            P(None, "seq", None, "batch"),
            P(None, "seq", None, "batch"),
            P(None, "seq", None, "batch"),
        ),
        out_specs=(
            P(None, "seq", None, "batch"),
            P(None, "seq", None, "batch"),
            P(None, "seq", None, "batch"),
            P("batch", "seq", None),
        ),
        check_vma=False,
    )
```

profile of v0, /device:TPU:0, one launch (start us, length us, event | category | flops | bytes accessed | tf_op | source)
XLA Modules:
  0.0 404.6 jit_solution(18138972879335876599)
XLA Ops:
  9.3 7.4 %all-to-all-start.3 = ((bf16[1,256,2,16,32]{1,4,2,0,3:T(8,128)(2,1)}), bf16[1,256,2,16,32]{1,4,2,0,3:T(8,128)(2,1)S(1)}, u32[]{:S(2)}, u32[]{:S(2)}) async-start(bf16[1,256,2,16,32]{1,4,2,0,3:T(8,128)(2,1)} %copy.145), calls=%async_computation.3 | async-start | bytes 1048576 | tf_op jit(solution)/shard_map/all_to_all | solution.py:81
  17.8 13.2 %all-to-all-done.3 = bf16[1,256,2,16,32]{1,4,2,0,3:T(8,128)(2,1)S(1)} async-done(((bf16[1,256,2,16,32]{1,4,2,0,3:T(8,128)(2,1)}), bf16[1,256,2,16,32]{1,4,2,0,3:T(8,128)(2,1)S(1)}, u32[]{:S(2)}, u32[]{:S(2)}) %all-to-all-start.3) | async-done | bytes 524320 | tf_op jit(solution)/shard_map/all_to_all | solution.py:81
  31.0 4.2 %all-to-all-start.2 = ((bf16[1,256,2,16,32]{1,4,2,0,3:T(8,128)(2,1)}), bf16[1,256,2,16,32]{1,4,2,0,3:T(8,128)(2,1)S(1)}, u32[]{:S(2)}, u32[]{:S(2)}) async-start(bf16[1,256,2,16,32]{1,4,2,0,3:T(8,128)(2,1)} %copy.140), calls=%async_computation.2 | async-start | bytes 1048576 | tf_op jit(solution)/shard_map/all_to_all | solution.py:80
  35.2 1.9 copy.136
  37.1 1.5 copy.137
  38.6 10.8 %all-to-all-done.2 = bf16[1,256,2,16,32]{1,4,2,0,3:T(8,128)(2,1)S(1)} async-done(((bf16[1,256,2,16,32]{1,4,2,0,3:T(8,128)(2,1)}), bf16[1,256,2,16,32]{1,4,2,0,3:T(8,128)(2,1)S(1)}, u32[]{:S(2)}, u32[]{:S(2)}) %all-to-all-start.2) | async-done | bytes 524320 | tf_op jit(solution)/shard_map/all_to_all | solution.py:80
  49.4 4.2 %all-to-all-start.1 = ((f32[2,2,256,16,32]{2,4,1,0,3:T(8,128)}), f32[2,2,256,16,32]{2,4,1,0,3:T(8,128)S(1)}, u32[]{:S(2)}, u32[]{:S(2)}) async-start(f32[2,2,256,16,32]{2,4,1,0,3:T(8,128)} %copy.137), calls=%async_computation.1 | async-start | bytes 4194304 | tf_op jit(solution)/shard_map/all_to_all | solution.py:88
  53.6 2.9 copy.155
  56.5 3.2 copy.156
  60.4 2.5 fusion.132
  62.8 2.4 fusion.137
  65.3 2.4 fusion.134
  67.6 26.9 %all-to-all-done.1 = f32[2,2,256,16,32]{2,4,1,0,3:T(8,128)S(1)} async-done(((f32[2,2,256,16,32]{2,4,1,0,3:T(8,128)}), f32[2,2,256,16,32]{2,4,1,0,3:T(8,128)S(1)}, u32[]{:S(2)}, u32[]{:S(2)}) %all-to-all-start.1) | async-done | bytes 2097184 | tf_op jit(solution)/shard_map/all_to_all | solution.py:88
  94.6 1.3 copy-done.1
  95.9 11.3 %all-to-all-start.4 = ((f32[2,2,256,16,32]{2,4,1,0,3:T(8,128)}), f32[2,2,256,16,32]{2,4,1,0,3:T(8,128)}, u32[]{:S(2)}, u32[]{:S(2)}) async-start(f32[2,2,256,16,32]{2,4,1,0,3:T(8,128)} %copy.156), calls=%async_computation.5 | async-start | bytes 4194304 | tf_op jit(solution)/shard_map/all_to_all | solution.py:91
  107.7 4.7 %fusion.35 = (f32[32,256,64]{1,0,2:T(8,128)S(1)}, f32[32,256,64]{1,0,2:T(8,128)S(1)}, f32[32,256,64]{1,0,2:T(8,128)S(1)}, f32[32,256,64]{1,0,2:T(8,128)S(1)}) fusion(f32[32,256,64]{1,0,2:T(8,128)} %fusion.134, f32[32,256]{1,0:T(8,128)S(1)} %get-tuple-element.35, f32[32,256]{1,0:T(8,128)S(1)} %get-tuple-element.36, f32[32,256,64]{1,0,2:T(8,128)} %fusion.137, ...), kind=kOutput, calls=%fused_computation.59 | convolution fusion | flops 108010496 | bytes 15269888 | tf_op jit(solution)/shard_map/ja,bach->bjch/dot_general | solution.py:29
  112.4 3.8 fusion.52
  116.2 3.8 fusion.50
  120.0 4.0 fusion.42
  124.0 3.8 fusion.44
  127.8 3.9 fusion.58
  131.7 4.2 %fusion.61 = f32[32,64,256]{2,1,0:T(8,128)S(1)} fusion(f32[32,64,256]{2,1,0:T(8,128)S(1)} %fusion.50, f32[32,256,64]{1,0,2:T(8,128)S(1)} %get-tuple-element.29), kind=kOutput, calls=%fused_computation.88 | convolution fusion | flops 1612054528 | bytes 6291456 | tf_op jit(solution)/shard_map/cm,bjch->bjmh/dot_general | solution.py:42
  135.9 3.8 fusion.67
  139.7 4.1 %fusion.26 = (f32[1,32,256,64]{2,3,1,0:T(8,128)S(1)}, f32[1,32,256,64]{2,3,1,0:T(8,128)S(1)}) fusion(f32[32,64,256]{2,1,0:T(8,128)S(1)} %fusion.61, f32[32,64,256]{2,1,0:T(8,128)S(1)} %fusion.67, f32[32,64,256]{2,1,0:T(8,128)S(1)} %fusion.58, f32[32,64,256]{2,1,0:T(8,128)S(1)} %fusion.44, f32[32,256,64]{1,0,2:T(8,128)S(1)} %get-tuple-element.34), kind=kOutput, calls=%fused_computation.38 | convolution fusion | flops 1615200256 | bytes 14680064 | tf_op jit(solution)/shard_map/cm,bjch->bjmh/dot_general | solution.py:37
  143.8 2.0 fusion
  145.8 2.9 copy.133
  148.7 3.2 copy.134
  151.9 7.6 %all-to-all-start = ((f32[2,2,256,16,32]{2,4,1,0,3:T(8,128)}), f32[2,2,256,16,32]{2,4,1,0,3:T(8,128)}, u32[]{:S(2)}, u32[]{:S(2)}) async-start(f32[2,2,256,16,32]{2,4,1,0,3:T(8,128)} %copy.134), calls=%async_computation | async-start | bytes 4194304 | tf_op jit(solution)/shard_map/all_to_all | solution.py:85
  159.5 1.8 multiply_bitcast_fusion.1
  161.3 1.5 copy.138
  162.8 1.8 multiply_bitcast_fusion
  164.6 1.5 copy.157
  166.1 34.5 %all-to-all-done = f32[2,2,256,16,32]{2,4,1,0,3:T(8,128)} async-done(((f32[2,2,256,16,32]{2,4,1,0,3:T(8,128)}), f32[2,2,256,16,32]{2,4,1,0,3:T(8,128)}, u32[]{:S(2)}, u32[]{:S(2)}) %all-to-all-start) | async-done | bytes 2097184 | tf_op jit(solution)/shard_map/all_to_all | solution.py:85
  200.5 3.2 copy.135
  203.7 6.5 %multiply_subtract_fusion = (f32[2,32,256,1,32]{2,4,1,0,3:T(8,128)S(1)}, f32[2,32,256,1,32]{2,4,1,0,3:T(8,128)}, f32[2,32,256,1,32]{2,4,1,0,3:T(8,128)}) fusion(f32[2,32,256,1,32]{2,4,1,0,3:T(8,128)} %bitcast.283, f32[2,32,256,1,32]{2,4,1,0,3:T(8,128)} %bitcast.281, bf16[2,32,256,1,32]{2,4,1,0,3:T(8,128)(2,1)} %reduce-scatter.2.cloned.1.call-done, ...), kind=kLoop, calls=%fused_computation.68 | loop fusion | flops 5242880 | bytes 13631488 | tf_op jit(solution)/shard_map/sub | solution.py:121
  210.2 1.5 copy.158
  211.7 11.3 %all-to-all-start.5 = ((f32[2,32,256,1,32]{2,4,0,3,1:T(8,128)}), f32[2,32,256,1,32]{2,4,0,3,1:T(8,128)}, u32[]{:S(2)}, u32[]{:S(2)}) async-start(f32[2,32,256,1,32]{2,4,0,3,1:T(8,128)} %copy.158), calls=%async_computation.6 | async-start | bytes 4194304 | tf_op jit(solution)/shard_map/all_to_all | solution.py:133
  223.0 3.2 copy.161
  226.2 37.8 %all-to-all-done.5 = f32[2,32,256,1,32]{2,4,0,3,1:T(8,128)} async-done(((f32[2,32,256,1,32]{2,4,0,3,1:T(8,128)}), f32[2,32,256,1,32]{2,4,0,3,1:T(8,128)}, u32[]{:S(2)}, u32[]{:S(2)}) %all-to-all-start.5) | async-done | bytes 2097184 | tf_op jit(solution)/shard_map/all_to_all | solution.py:133
  264.0 11.3 %all-to-all-start.6 = ((f32[2,32,256,1,32]{2,4,0,3,1:T(8,128)}), f32[2,32,256,1,32]{2,4,0,3,1:T(8,128)}, u32[]{:S(2)}, u32[]{:S(2)}) async-start(f32[2,32,256,1,32]{2,4,0,3,1:T(8,128)} %copy.161), calls=%async_computation.7 | async-start | bytes 4194304 | tf_op jit(solution)/shard_map/all_to_all | solution.py:136
  275.4 5.5 %fusion.8 = f32[2,32,256,32]{2,3,1,0:T(8,128)} fusion(f32[2,32,256,32]{2,3,1,0:T(8,128)} %bitcast.284, f32[2,32,256,32]{2,3,1,0:T(8,128)} %bitcast.280, bf16[2,32,256,1,32]{2,4,1,0,3:T(8,128)(2,1)S(1)} %copy-done.2, f32[2,32,256,32]{2,3,1,0:T(8,128)} %bitcast.282), kind=kLoop, calls=%fused_computation.14 | loop fusion | flops 5242880 | bytes 9437184 | tf_op jit(solution)/shard_map/sub | solution.py:121
  280.9 3.2 copy.164
  284.0 32.3 %all-to-all-done.6 = f32[2,32,256,1,32]{2,4,0,3,1:T(8,128)} async-done(((f32[2,32,256,1,32]{2,4,0,3,1:T(8,128)}), f32[2,32,256,1,32]{2,4,0,3,1:T(8,128)}, u32[]{:S(2)}, u32[]{:S(2)}) %all-to-all-start.6) | async-done | bytes 2097184 | tf_op jit(solution)/shard_map/all_to_all | solution.py:136
  316.3 11.4 %all-to-all-start.7 = ((f32[2,32,256,1,32]{2,4,0,3,1:T(8,128)}), f32[2,32,256,1,32]{2,4,0,3,1:T(8,128)}, u32[]{:S(2)}, u32[]{:S(2)}) async-start(f32[2,32,256,1,32]{2,4,0,3,1:T(8,128)} %copy.164), calls=%async_computation.8 | async-start | bytes 4194304 | tf_op jit(solution)/shard_map/all_to_all | solution.py:139
  327.8 11.3 %all-gather.2.cloned.1.call-done = f32[2,32,256,64]{2,3,1,0:T(8,128)} async-done(((f32[2,32,256,32]{2,3,1,0:T(8,128)}), f32[2,32,256,64]{2,3,1,0:T(8,128)}) %all-gather.2.cloned.1.call-update) | async-done | bytes 4194320 | tf_op jit(solution)/shard_map/all_gather | solution.py:122
  339.0 3.7 fusion.28
  342.8 2.8 fusion.20
  345.6 2.8 fusion.18
  348.5 2.9 fusion.70
  351.4 3.4 fusion.15
  354.8 2.4 fusion.38
  357.3 2.5 fusion.85
  360.0 2.8 copy.172
  362.8 2.7 reshape.247
  365.4 3.2 all-to-all-done.7
  368.6 11.2 %all-to-all-start.8 = ((bf16[16,2,8192]{2,1,0:T(2,128)(2,1)}), bf16[16,2,8192]{2,1,0:T(2,128)(2,1)S(1)}, u32[]{:S(2)}, u32[]{:S(2)}) async-start(bf16[16,2,8192]{2,1,0:T(2,128)(2,1)} %reshape.247), calls=%async_computation.9 | async-start | bytes 1048576 | tf_op jit(solution)/shard_map/all_to_all | solution.py:143
  379.9 1.7 copy.159
  381.7 1.8 copy.175
  383.6 1.7 copy.162
  385.4 1.8 copy.176
  387.2 1.7 copy.165
  389.1 1.8 copy.177
  390.9 3.2 all-to-all-done.8
  395.2 1.3 copy.181
  (26 shorter events, 7.2 us)
Async XLA Ops:
  7.2 9.5 %copy-start.3 = (bf16[1,256,1024]{2,1,0:T(8,128)(2,1)S(1)}, bf16[1,256,1024]{2,1,0:T(8,128)(2,1)}, u32[]{:S(2)}) copy-start(bf16[1,256,1024]{2,1,0:T(8,128)(2,1)} %param.5) | copy-start | bytes 1572868
  9.3 21.7 %all-to-all-start.3 = ((bf16[1,256,2,16,32]{1,4,2,0,3:T(8,128)(2,1)}), bf16[1,256,2,16,32]{1,4,2,0,3:T(8,128)(2,1)S(1)}, u32[]{:S(2)}, u32[]{:S(2)}) async-start(bf16[1,256,2,16,32]{1,4,2,0,3:T(8,128)(2,1)} %copy.145), calls=%async_computation.3 | async-start | bytes 1048576 | tf_op jit(solution)/shard_map/all_to_all | solution.py:81
  31.0 18.4 %all-to-all-start.2 = ((bf16[1,256,2,16,32]{1,4,2,0,3:T(8,128)(2,1)}), bf16[1,256,2,16,32]{1,4,2,0,3:T(8,128)(2,1)S(1)}, u32[]{:S(2)}, u32[]{:S(2)}) async-start(bf16[1,256,2,16,32]{1,4,2,0,3:T(8,128)(2,1)} %copy.140), calls=%async_computation.2 | async-start | bytes 1048576 | tf_op jit(solution)/shard_map/all_to_all | solution.py:80
  49.4 45.1 %all-to-all-start.1 = ((f32[2,2,256,16,32]{2,4,1,0,3:T(8,128)}), f32[2,2,256,16,32]{2,4,1,0,3:T(8,128)S(1)}, u32[]{:S(2)}, u32[]{:S(2)}) async-start(f32[2,2,256,16,32]{2,4,1,0,3:T(8,128)} %copy.137), calls=%async_computation.1 | async-start | bytes 4194304 | tf_op jit(solution)/shard_map/all_to_all | solution.py:88
  94.6 1.3 copy-start.1
  95.9 56.0 %all-to-all-start.4 = ((f32[2,2,256,16,32]{2,4,1,0,3:T(8,128)}), f32[2,2,256,16,32]{2,4,1,0,3:T(8,128)}, u32[]{:S(2)}, u32[]{:S(2)}) async-start(f32[2,2,256,16,32]{2,4,1,0,3:T(8,128)} %copy.156), calls=%async_computation.5 | async-start | bytes 4194304 | tf_op jit(solution)/shard_map/all_to_all | solution.py:91
  107.2 96.5 %reduce-scatter.2.cloned.1.call-start = ((), (), s32[]{:S(2)}) async-start(), calls=%async_computation.10 | async-start | bytes 3145728 | tf_op jit(solution)/shard_map/reduce_scatter | solution.py:115
  135.9 3.8 copy-start
  151.9 48.6 %all-to-all-start = ((f32[2,2,256,16,32]{2,4,1,0,3:T(8,128)}), f32[2,2,256,16,32]{2,4,1,0,3:T(8,128)}, u32[]{:S(2)}, u32[]{:S(2)}) async-start(f32[2,2,256,16,32]{2,4,1,0,3:T(8,128)} %copy.134), calls=%async_computation | async-start | bytes 4194304 | tf_op jit(solution)/shard_map/all_to_all | solution.py:85
  211.7 52.3 %all-to-all-start.5 = ((f32[2,32,256,1,32]{2,4,0,3,1:T(8,128)}), f32[2,32,256,1,32]{2,4,0,3,1:T(8,128)}, u32[]{:S(2)}, u32[]{:S(2)}) async-start(f32[2,32,256,1,32]{2,4,0,3,1:T(8,128)} %copy.158), calls=%async_computation.6 | async-start | bytes 4194304 | tf_op jit(solution)/shard_map/all_to_all | solution.py:133
  226.2 49.2 %copy-start.2 = (bf16[2,32,256,1,32]{2,4,1,0,3:T(8,128)(2,1)S(1)}, bf16[2,32,256,1,32]{2,4,1,0,3:T(8,128)(2,1)}, u32[]{:S(2)}) copy-start(bf16[2,32,256,1,32]{2,4,1,0,3:T(8,128)(2,1)} %reduce-scatter.2.cloned.1.call-done) | copy-start | bytes 3145732
  264.0 52.3 %all-to-all-start.6 = ((f32[2,32,256,1,32]{2,4,0,3,1:T(8,128)}), f32[2,32,256,1,32]{2,4,0,3,1:T(8,128)}, u32[]{:S(2)}, u32[]{:S(2)}) async-start(f32[2,32,256,1,32]{2,4,0,3,1:T(8,128)} %copy.161), calls=%async_computation.7 | async-start | bytes 4194304 | tf_op jit(solution)/shard_map/all_to_all | solution.py:136
  275.3 63.7 %all-gather.2.cloned.1.call-start = ((), (), s32[]{:S(2)}) async-start(), calls=%async_computation.11 | async-start | bytes 6291456 | tf_op jit(solution)/shard_map/all_gather | solution.py:122
  316.3 52.3 %all-to-all-start.7 = ((f32[2,32,256,1,32]{2,4,0,3,1:T(8,128)}), f32[2,32,256,1,32]{2,4,0,3,1:T(8,128)}, u32[]{:S(2)}, u32[]{:S(2)}) async-start(f32[2,32,256,1,32]{2,4,0,3,1:T(8,128)} %copy.164), calls=%async_computation.8 | async-start | bytes 4194304 | tf_op jit(solution)/shard_map/all_to_all | solution.py:139
  368.6 25.5 %all-to-all-start.8 = ((bf16[16,2,8192]{2,1,0:T(2,128)(2,1)}), bf16[16,2,8192]{2,1,0:T(2,128)(2,1)S(1)}, u32[]{:S(2)}, u32[]{:S(2)}) async-start(bf16[16,2,8192]{2,1,0:T(2,128)(2,1)} %reshape.247), calls=%async_computation.9 | async-start | bytes 1048576 | tf_op jit(solution)/shard_map/all_to_all | solution.py:143
Sparse Core Ops, SparseCore 0:
  145.9 33.1 reduce-scatter.1
  281.0 58.0 all-gather.1
where the time goes:
time: 410 us; the launch traced here: 405 us
  waiting for transfers between devices  173 us (42%)
  starting transfers between devices  80.3 us (20%)
  matrix products  60.2 us (15%)
  local copies, waits for them, and re-layouts  54.6 us (13%)
  other arithmetic  21.5 us (5%)
  between operations  14.6 us (4%)
    all_to_all x1, waiting for transfers between devices, channel_layout(): lax.all_to_all(new_spectrum.reshape(back_shape), 'seq', split_axis=1, con...  37.8 us
    all_to_all x1, waiting for transfers between devices, channel_layout(): lax.all_to_all(spectrum.reshape(state_shape), 'seq', split_axis=3, concat...  34.5 us
    all_to_all x1, waiting for transfers between devices, channel_layout(): lax.all_to_all(new_first.reshape(back_shape), 'seq', split_axis=1, concat...  32.3 us
    all_to_all x1, waiting for transfers between devices, channel_layout(): lax.all_to_all(first_moment.reshape(state_shape), 'seq', split_axis=3, co...  26.9 us
    unnamed x19, local copies, waits for them, and re-layouts  20.7 us
    all_to_all x1, waiting for transfers between devices, channel_layout(): lax.all_to_all(cotangent_parts, 'seq', split_axis=3, concat_axis=1, tiled...  13.2 us
    sub x2, other arithmetic, channel_layout(): spec_cols - step_rate * jnp.tanh(new_first / (jnp.sqrt(new_second) + epsi...  12 us
    all_to_all x1, starting transfers between devices, channel_layout(): lax.all_to_all(new_second.reshape(back_shape), 'seq', split_axis=1, conca...  11.4 us
  transfers between devices with their start and end apart: 11, of which 9 were waited for; matrix products, arithmetic and copies ran while one was open for 30% of the time, Pallas kernels for 0%

commit v1 on v0

--- a/solution.py
+++ b/solution.py
@@ -3,10 +3,25 @@
 import jax.numpy as jnp
 from jax import lax
 from jax.sharding import PartitionSpec as P
+from jax.lax import axis_index, ppermute, psum
 
 full_turn = 2.0 * math.pi
 step_rate = 0.5
 epsilon = 1e-06
+
+
+def change_face(local_array, ndim_at, array_in):
+    oldest = local_array.shape
+    newest = local_array.reshape(
+        *oldest[:ndim_at], array_in, oldest[ndim_at] // array_in, *oldest[ndim_at + 1 :]
+    )
+    return jnp.moveaxis(newest, ndim_at, 0)
+
+
+def tiles_obtain(vals, array_dim):
+    inter = list(vals.shape[1:])
+    inter[array_dim] *= vals.shape[0]
+    return jnp.moveaxis(vals, 0, array_dim).reshape(inter)
 
 
 def angles(numer, modulus):
@@ -129,13 +144,30 @@
         batch_rows, seq_count * point_count, batch_count, 1, narrow
     )
     back_shape = (2, outer_count, point_count, 1, narrow)
+
+    def clear_the_space(local_block, named_axis, array_here, patch):
+        main = psum(1, axis_name=named_axis)
+        z_new = axis_index(named_axis)
+        parts_out, last = (main, z_new)
+        z2 = change_face(local_block, array_here, parts_out)
+        row_list = [z2[last]]
+        for w in [*range(1, parts_out)]:
+            arr_now = z2[(last + w) % parts_out]
+            part_next = ppermute(
+                arr_now,
+                axis_name=named_axis,
+                perm=[(s, (s + w) % parts_out) for s in range(parts_out)],
+            )
+            row_list.append(part_next)
+        high = jnp.stack(row_list, axis=0)
+        z2 = high[(last - jnp.arange(parts_out)) % parts_out]
+        return tiles_obtain(z2, patch)
+
     spec_back, first_back, second_back = (
         lax.all_to_all(
             new_spectrum.reshape(back_shape), "seq", split_axis=1, concat_axis=3, tiled=True
         ),
-        lax.all_to_all(
-            new_first.reshape(back_shape), "seq", split_axis=1, concat_axis=3, tiled=True
-        ),
+        clear_the_space(new_first.reshape(back_shape), "seq", 1, 3),
         lax.all_to_all(
             new_second.reshape(back_shape), "seq", split_axis=1, concat_axis=3, tiled=True
         ),

time: 410 us -> 441 us (1.076)
  starting transfers between devices: 80.3 us -> 131 us
  waiting for transfers between devices: 173 us -> 130 us
  local copies, waits for them, and re-layouts: 54.6 us -> 75.6 us
    ppermute x0 -> x15, starting transfers between devices: none -> 67.3 us  [clear_the_space(): ppermute(arr_now, axis_name=named_axis, perm=[(s, (s + w) % parts_out) fo...]
    ppermute x0 -> x15, waiting for transfers between devices: none -> 43.2 us  [clear_the_space(): ppermute(arr_now, axis_name=named_axis, perm=[(s, (s + w) % parts_out) fo...]
    all_to_all x1, waiting for transfers between devices: 37.8 us -> 0.01 us  [channel_layout(): lax.all_to_all(new_spectrum.reshape(back_shape), 'seq', split_axis=1, con...]
    all_to_all x1 -> x0, waiting for transfers between devices: 32.3 us -> none  [channel_layout(): lax.all_to_all(new_first.reshape(back_shape), 'seq', split_axis=1, concat...]
    unnamed x19 -> x42, local copies, waits for them, and re-layouts: 20.7 us -> 38.3 us
    all_to_all x1 -> x0, starting transfers between devices: 11.3 us -> none  [channel_layout(): lax.all_to_all(new_first.reshape(back_shape), 'seq', split_axis=1, concat...]
    all_gather x1, waiting for transfers between devices: 11.3 us -> 0.02 us  [channel_layout(): group_filter = lax.all_gather(new_spectrum, 'batch', axis=3, tiled=True)]
    add x0 -> x2, other arithmetic: none -> 8.6 us  [the longest x1 6.54 us: channel_layout(): new_second = 0.99 * second_cols + 0.01 * own_grad * own_grad]
  transfers between devices with their start and end apart: 11 -> 25, of which waited for: 9 -> 7; matrix products, arithmetic and copies ran while one was open for 30% -> 33% of each run, Pallas kernels for 0% -> 0%
where the time goes in v1:
time: 441 us; the launch traced here: 435 us
  starting transfers between devices  131 us (30%)
  waiting for transfers between devices  130 us (29%)
  local copies, waits for them, and re-layouts  75.6 us (17%)
  matrix products  59.9 us (14%)
  other arithmetic  22.7 us (5%)
  between operations  15 us (3%)
    ppermute x15, starting transfers between devices, clear_the_space(): ppermute(arr_now, axis_name=named_axis, perm=[(s, (s + w) % parts_out) fo...  67.3 us
    ppermute x15, waiting for transfers between devices, clear_the_space(): ppermute(arr_now, axis_name=named_axis, perm=[(s, (s + w) % parts_out) fo...  43.2 us
    unnamed x42, local copies, waits for them, and re-layouts  38.3 us
    all_to_all x1, waiting for transfers between devices, channel_layout(): lax.all_to_all(spectrum.reshape(state_shape), 'seq', split_axis=3, concat...  35.9 us
    all_to_all x1, waiting for transfers between devices, channel_layout(): lax.all_to_all(first_moment.reshape(state_shape), 'seq', split_axis=3, co...  27 us
    all_to_all x1, starting transfers between devices, channel_layout(): lax.all_to_all(new_second.reshape(back_shape), 'seq', split_axis=1, conca...  13.4 us
    all_to_all x1, waiting for transfers between devices, channel_layout(): lax.all_to_all(cotangent_parts, 'seq', split_axis=3, concat_axis=1, tiled...  13.2 us
    all_to_all x1, starting transfers between devices, channel_layout(): lax.all_to_all(new_spectrum.reshape(back_shape), 'seq', split_axis=1, con...  11.4 us
  transfers between devices with their start and end apart: 25, of which 7 were waited for; matrix products, arithmetic and copies ran while one was open for 33% of the time, Pallas kernels for 0%

profile of v1, /device:TPU:0, one launch (start us, length us, event | category | flops | bytes accessed | tf_op | source)
XLA Modules:
  0.0 434.9 jit_solution(91584089899371282)
XLA Ops:
  9.3 7.4 %all-to-all-start.3 = ((bf16[1,256,2,16,32]{1,4,2,0,3:T(8,128)(2,1)}), bf16[1,256,2,16,32]{1,4,2,0,3:T(8,128)(2,1)S(1)}, u32[]{:S(2)}, u32[]{:S(2)}) async-start(bf16[1,256,2,16,32]{1,4,2,0,3:T(8,128)(2,1)} %copy.147), calls=%async_computation.3 | async-start | bytes 1048576 | tf_op jit(solution)/shard_map/all_to_all | solution.py:96
  17.8 13.2 %all-to-all-done.3 = bf16[1,256,2,16,32]{1,4,2,0,3:T(8,128)(2,1)S(1)} async-done(((bf16[1,256,2,16,32]{1,4,2,0,3:T(8,128)(2,1)}), bf16[1,256,2,16,32]{1,4,2,0,3:T(8,128)(2,1)S(1)}, u32[]{:S(2)}, u32[]{:S(2)}) %all-to-all-start.3) | async-done | bytes 524320 | tf_op jit(solution)/shard_map/all_to_all | solution.py:96
  31.0 4.2 all-to-all-start.2
  35.2 1.9 copy.138
  37.1 1.6 copy.139
  38.7 10.8 %all-to-all-done.2 = bf16[1,256,2,16,32]{1,4,2,0,3:T(8,128)(2,1)S(1)} async-done(((bf16[1,256,2,16,32]{1,4,2,0,3:T(8,128)(2,1)}), bf16[1,256,2,16,32]{1,4,2,0,3:T(8,128)(2,1)S(1)}, u32[]{:S(2)}, u32[]{:S(2)}) %all-to-all-start.2) | async-done | bytes 524320 | tf_op jit(solution)/shard_map/all_to_all | solution.py:95
  49.4 4.2 all-to-all-start.1
  53.6 2.9 copy.157
  56.5 3.2 copy.158
  60.4 2.4 fusion.131
  62.8 2.4 fusion.136
  65.2 2.4 fusion.133
  67.6 27.0 %all-to-all-done.1 = f32[2,2,256,16,32]{2,4,1,0,3:T(8,128)S(1)} async-done(((f32[2,2,256,16,32]{2,4,1,0,3:T(8,128)}), f32[2,2,256,16,32]{2,4,1,0,3:T(8,128)S(1)}, u32[]{:S(2)}, u32[]{:S(2)}) %all-to-all-start.1) | async-done | bytes 2097184 | tf_op jit(solution)/shard_map/all_to_all | solution.py:103
  94.6 11.3 %all-to-all-start.4 = ((f32[2,2,256,16,32]{2,4,1,0,3:T(8,128)}), f32[2,2,256,16,32]{2,4,1,0,3:T(8,128)}, u32[]{:S(2)}, u32[]{:S(2)}) async-start(f32[2,2,256,16,32]{2,4,1,0,3:T(8,128)} %copy.158), calls=%async_computation.5 | async-start | bytes 4194304 | tf_op jit(solution)/shard_map/all_to_all | solution.py:106
  106.4 4.7 %fusion.34 = (f32[32,256,64]{1,0,2:T(8,128)S(1)}, f32[32,256,64]{1,0,2:T(8,128)S(1)}, f32[32,256,64]{1,0,2:T(8,128)S(1)}, f32[32,256,64]{1,0,2:T(8,128)S(1)}) fusion(f32[32,256,64]{1,0,2:T(8,128)} %fusion.133, f32[32,256]{1,0:T(8,128)S(1)} %get-tuple-element.50, f32[32,256]{1,0:T(8,128)S(1)} %get-tuple-element.51, f32[32,256,64]{1,0,2:T(8,128)} %fusion.136, ...), kind=kOutput, calls=%fused_computation.59 | convolution fusion | flops 108010496 | bytes 15269888 | tf_op jit(solution)/shard_map/ja,bach->bjch/dot_general | solution.py:44
  111.1 3.8 fusion.51
  114.9 3.8 fusion.49
  118.7 4.0 fusion.41
  122.7 3.8 fusion.43
  126.5 3.9 fusion.57
  130.3 4.0 fusion.60
  134.4 3.8 fusion.66
  138.2 4.1 fusion.25
  142.3 1.9 fusion
  144.2 2.9 copy.135
  147.1 3.2 copy.136
  150.3 8.2 %all-to-all-start = ((f32[2,2,256,16,32]{2,4,1,0,3:T(8,128)}), f32[2,2,256,16,32]{2,4,1,0,3:T(8,128)}, u32[]{:S(2)}, u32[]{:S(2)}) async-start(f32[2,2,256,16,32]{2,4,1,0,3:T(8,128)} %copy.136), calls=%async_computation | async-start | bytes 4194304 | tf_op jit(solution)/shard_map/all_to_all | solution.py:100
  160.3 1.9 multiply_bitcast_fusion
  163.7 35.9 %all-to-all-done = f32[2,2,256,16,32]{2,4,1,0,3:T(8,128)} async-done(((f32[2,2,256,16,32]{2,4,1,0,3:T(8,128)}), f32[2,2,256,16,32]{2,4,1,0,3:T(8,128)}, u32[]{:S(2)}, u32[]{:S(2)}) %all-to-all-start) | async-done | bytes 2097184 | tf_op jit(solution)/shard_map/all_to_all | solution.py:100
  199.6 3.2 copy.137
  202.7 6.5 %fusion.12 = (f32[2,32,256,1,32]{2,4,1,0,3:T(8,128)}, f32[2,32,256,1,32]{2,4,1,0,3:T(8,128)S(1)}, f32[2,32,256,1,32]{2,4,1,0,3:T(8,128)}) fusion(f32[2,32,256,1,32]{2,4,1,0,3:T(8,128)} %bitcast.351, bf16[2,32,256,1,32]{2,4,1,0,3:T(8,128)(2,1)} %reduce-scatter.2.cloned.1.call-done, f32[2,32,256,1,32]{2,4,1,0,3:T(8,128)} %bitcast.353, ...), kind=kLoop, calls=%fused_computation.19 | loop fusion | flops 5242880 | bytes 13631488 | tf_op jit(solution)/shard_map/add | solution.py:135
  210.7 11.4 %all-to-all-start.5 = ((f32[2,32,256,1,32]{2,4,0,3,1:T(8,128)}), f32[2,32,256,1,32]{2,4,0,3,1:T(8,128)}, u32[]{:S(2)}, u32[]{:S(2)}) async-start(f32[2,32,256,1,32]{2,4,0,3,1:T(8,128)} %copy.160), calls=%async_computation.6 | async-start | bytes 4194304 | tf_op jit(solution)/shard_map/all_to_all | solution.py:167
  222.2 5.6 %fusion.8 = f32[2,32,256,32]{2,3,1,0:T(8,128)} fusion(f32[2,32,256,32]{2,3,1,0:T(8,128)} %bitcast.354, f32[2,32,256,32]{2,3,1,0:T(8,128)} %bitcast.350, bf16[2,32,256,1,32]{2,4,1,0,3:T(8,128)(2,1)S(1)} %copy-done.5, f32[2,32,256,32]{2,3,1,0:T(8,128)} %bitcast.352), kind=kLoop, calls=%fused_computation.15 | loop fusion | flops 5242880 | bytes 9437184 | tf_op jit(solution)/shard_map/sub | solution.py:136
  228.0 2.1 copy_add_fusion
  232.7 1.6 collective-permute-start.1
  234.3 2.3 collective-permute-start.2
  240.7 23.6 %collective-permute-done = f32[2,2,256,1,32]{2,4,1,0,3:T(8,128)} collective-permute-done((f32[2,2,256,1,32]{2,4,1,0,3:T(8,128)}, f32[2,2,256,1,32]{2,4,1,0,3:T(8,128)}, u32[]{:S(2)}, u32[]{:S(2)}) %collective-permute-start) | collective-permute-done | bytes 131104 | tf_op jit(solution)/shard_map/ppermute | solution.py:156
  265.3 14.5 %collective-permute-start.6 = (f32[2,2,256,1,32]{2,4,1,0,3:T(8,128)S(1)}, f32[2,2,256,1,32]{2,4,1,0,3:T(8,128)}, u32[]{:S(2)}, u32[]{:S(2)}) collective-permute-start(f32[2,2,256,1,32]{2,4,1,0,3:T(8,128)S(1)} %get-tuple-element.40), channel_id=1, source_target_pairs={{0,14},{2,16},{4,18},{6,20},{8,22},{10,24},{12,26},{14,28},{16,30}... | collective-permute-start | bytes 393224 | tf_op jit(solution)/shard_map/ppermute | solution.py:156
  281.0 2.4 collective-permute-start.8
  283.3 13.4 %all-to-all-start.6 = ((f32[2,32,256,1,32]{2,4,0,3,1:T(8,128)}), f32[2,32,256,1,32]{2,4,0,3,1:T(8,128)}, u32[]{:S(2)}, u32[]{:S(2)}) async-start(f32[2,32,256,1,32]{2,4,0,3,1:T(8,128)} %copy.165), calls=%async_computation.7 | async-start | bytes 4194304 | tf_op jit(solution)/shard_map/all_to_all | solution.py:171
  297.7 3.7 collective-permute-start.9
  303.3 2.2 collective-permute-start.11
  306.4 1.8 collective-permute-start.12
  308.2 8.8 %collective-permute-start.13 = (f32[2,2,256,1,32]{2,4,1,0,3:T(8,128)S(1)}, f32[2,2,256,1,32]{2,4,1,0,3:T(8,128)}, u32[]{:S(2)}, u32[]{:S(2)}) collective-permute-start(f32[2,2,256,1,32]{2,4,1,0,3:T(8,128)S(1)} %get-tuple-element.33), channel_id=1, source_target_pairs={{0,28},{2,30},{4,0},{6,2},{8,4},{10,6},{12,8},{14,10},{16,12},{18,... | collective-permute-start | bytes 393224 | tf_op jit(solution)/shard_map/ppermute | solution.py:156
  317.0 19.5 %collective-permute-done.9 = f32[2,2,256,1,32]{2,4,1,0,3:T(8,128)S(1)} collective-permute-done((f32[2,2,256,1,32]{2,4,1,0,3:T(8,128)S(1)}, f32[2,2,256,1,32]{2,4,1,0,3:T(8,128)S(1)}, u32[]{:S(2)}, u32[]{:S(2)}) %collective-permute-start.9) | collective-permute-done | bytes 131104 | tf_op jit(solution)/shard_map/ppermute | solution.py:156
  336.5 27.7 %collective-permute-start.14 = (f32[2,2,256,1,32]{2,4,1,0,3:T(8,128)S(1)}, f32[2,2,256,1,32]{2,4,1,0,3:T(8,128)}, u32[]{:S(2)}, u32[]{:S(2)}) collective-permute-start(f32[2,2,256,1,32]{2,4,1,0,3:T(8,128)S(1)} %get-tuple-element.32), channel_id=1, source_target_pairs={{0,30},{2,0},{4,2},{6,4},{8,6},{10,8},{12,10},{14,12},{16,14},{18,... | collective-permute-start | bytes 393224 | tf_op jit(solution)/shard_map/ppermute | solution.py:156
  364.3 4.3 fusion.27
  368.6 2.8 fusion.19
  371.5 2.8 fusion.17
  374.3 2.9 fusion.69
  377.2 3.4 fusion.14
  380.7 2.4 fusion.37
  383.1 2.5 fusion.84
  385.8 3.8 copy.173
  389.7 5.9 %reshape.344 = bf16[16,2,8192]{2,1,0:T(2,128)(2,1)} reshape(bf16[4096,1,1,2,32]{4,3,2,1,0:T(2,128)(2,1)} %bitcast.357) | data formatting | bytes 1048576
  395.6 3.6 all-to-all-start.7
  405.1 2.3 gather_fusion
  409.0 2.9 copy.177
  411.8 1.8 copy.161
  413.7 1.6 copy.162
  415.2 2.9 copy.176
  418.1 1.8 copy.166
  420.0 1.6 copy.167
  421.6 2.9 copy.178
  (81 shorter events, 32.9 us)
Async XLA Ops:
  7.2 9.5 %copy-start.6 = (bf16[1,256,1024]{2,1,0:T(8,128)(2,1)S(1)}, bf16[1,256,1024]{2,1,0:T(8,128)(2,1)}, u32[]{:S(2)}) copy-start(bf16[1,256,1024]{2,1,0:T(8,128)(2,1)} %param.5) | copy-start | bytes 1572868
  9.3 21.7 %all-to-all-start.3 = ((bf16[1,256,2,16,32]{1,4,2,0,3:T(8,128)(2,1)}), bf16[1,256,2,16,32]{1,4,2,0,3:T(8,128)(2,1)S(1)}, u32[]{:S(2)}, u32[]{:S(2)}) async-start(bf16[1,256,2,16,32]{1,4,2,0,3:T(8,128)(2,1)} %copy.147), calls=%async_computation.3 | async-start | bytes 1048576 | tf_op jit(solution)/shard_map/all_to_all | solution.py:96
  31.0 18.4 %all-to-all-start.2 = ((bf16[1,256,2,16,32]{1,4,2,0,3:T(8,128)(2,1)}), bf16[1,256,2,16,32]{1,4,2,0,3:T(8,128)(2,1)S(1)}, u32[]{:S(2)}, u32[]{:S(2)}) async-start(bf16[1,256,2,16,32]{1,4,2,0,3:T(8,128)(2,1)} %copy.142), calls=%async_computation.2 | async-start | bytes 1048576 | tf_op jit(solution)/shard_map/all_to_all | solution.py:95
  49.4 45.1 %all-to-all-start.1 = ((f32[2,2,256,16,32]{2,4,1,0,3:T(8,128)}), f32[2,2,256,16,32]{2,4,1,0,3:T(8,128)S(1)}, u32[]{:S(2)}, u32[]{:S(2)}) async-start(f32[2,2,256,16,32]{2,4,1,0,3:T(8,128)} %copy.139), calls=%async_computation.1 | async-start | bytes 4194304 | tf_op jit(solution)/shard_map/all_to_all | solution.py:103
  94.6 55.8 %all-to-all-start.4 = ((f32[2,2,256,16,32]{2,4,1,0,3:T(8,128)}), f32[2,2,256,16,32]{2,4,1,0,3:T(8,128)}, u32[]{:S(2)}, u32[]{:S(2)}) async-start(f32[2,2,256,16,32]{2,4,1,0,3:T(8,128)} %copy.158), calls=%async_computation.5 | async-start | bytes 4194304 | tf_op jit(solution)/shard_map/all_to_all | solution.py:106
  105.8 96.9 %reduce-scatter.2.cloned.1.call-start = ((), (), s32[]{:S(2)}) async-start(), calls=%async_computation.9 | async-start | bytes 3145728 | tf_op jit(solution)/shard_map/reduce_scatter | solution.py:130
  130.3 7.8 %copy-start.1 = (f32[32,64,256]{2,1,0:T(8,128)}, f32[32,64,256]{2,1,0:T(8,128)S(1)}, u32[]{:S(2)}) copy-start(f32[32,64,256]{2,1,0:T(8,128)S(1)} %fusion.57) | copy-start | bytes 6291460
  134.3 3.8 copy-start.2
  150.3 49.2 %all-to-all-start = ((f32[2,2,256,16,32]{2,4,1,0,3:T(8,128)}), f32[2,2,256,16,32]{2,4,1,0,3:T(8,128)}, u32[]{:S(2)}, u32[]{:S(2)}) async-start(f32[2,2,256,16,32]{2,4,1,0,3:T(8,128)} %copy.136), calls=%async_computation | async-start | bytes 4194304 | tf_op jit(solution)/shard_map/all_to_all | solution.py:100
  210.7 11.5 %copy-start.5 = (bf16[2,32,256,1,32]{2,4,1,0,3:T(8,128)(2,1)S(1)}, bf16[2,32,256,1,32]{2,4,1,0,3:T(8,128)(2,1)}, u32[]{:S(2)}) copy-start(bf16[2,32,256,1,32]{2,4,1,0,3:T(8,128)(2,1)} %reduce-scatter.2.cloned.1.call-done) | copy-start | bytes 3145732
  210.7 72.6 %all-to-all-start.5 = ((f32[2,32,256,1,32]{2,4,0,3,1:T(8,128)}), f32[2,32,256,1,32]{2,4,0,3,1:T(8,128)}, u32[]{:S(2)}, u32[]{:S(2)}) async-start(f32[2,32,256,1,32]{2,4,0,3,1:T(8,128)} %copy.160), calls=%async_computation.6 | async-start | bytes 4194304 | tf_op jit(solution)/shard_map/all_to_all | solution.py:167
  222.1 142.2 %all-gather.2.cloned.1.call-start = ((), (), s32[]{:S(2)}) async-start(), calls=%async_computation.10 | async-start | bytes 6291456 | tf_op jit(solution)/shard_map/all_gather | solution.py:137
  230.1 1.3 copy-start.3
  231.4 6.8 %copy-start.4 = (f32[2,32,256,1,32]{2,4,1,0,3:T(8,128)S(1)}, f32[2,32,256,1,32]{2,4,1,0,3:T(8,128)}, u32[]{:S(2)}) copy-start(f32[2,32,256,1,32]{2,4,1,0,3:T(8,128)} %get-tuple-element.30) | copy-start | bytes 6291460
  232.3 31.9 %collective-permute-start = (f32[2,2,256,1,32]{2,4,1,0,3:T(8,128)}, f32[2,2,256,1,32]{2,4,1,0,3:T(8,128)}, u32[]{:S(2)}, u32[]{:S(2)}) collective-permute-start(f32[2,2,256,1,32]{2,4,1,0,3:T(8,128)} %get-tuple-element.46), channel_id=1, source_target_pairs={{0,2},{2,4},{4,6},{6,8},{8,10},{10,12},{12,14},{14,16},{16,18},{18... | collective-permute-start | bytes 393224 | tf_op jit(solution)/shard_map/ppermute | solution.py:156
  232.7 32.6 %collective-permute-start.1 = (f32[2,2,256,1,32]{2,4,1,0,3:T(8,128)}, f32[2,2,256,1,32]{2,4,1,0,3:T(8,128)S(1)}, u32[]{:S(2)}, u32[]{:S(2)}) collective-permute-start(f32[2,2,256,1,32]{2,4,1,0,3:T(8,128)} %get-tuple-element.45), channel_id=1, source_target_pairs={{0,4},{2,6},{4,8},{6,10},{8,12},{10,14},{12,16},{14,18},{16,20},{1... | collective-permute-start | bytes 393224 | tf_op jit(solution)/shard_map/ppermute | solution.py:156
  234.3 45.4 %collective-permute-start.2 = (f32[2,2,256,1,32]{2,4,1,0,3:T(8,128)S(1)}, f32[2,2,256,1,32]{2,4,1,0,3:T(8,128)S(1)}, u32[]{:S(2)}, u32[]{:S(2)}) collective-permute-start(f32[2,2,256,1,32]{2,4,1,0,3:T(8,128)S(1)} %get-tuple-element.44), channel_id=1, source_target_pairs={{0,6},{2,8},{4,10},{6,12},{8,14},{10,16},{12,18},{14,20},{16,22},{... | collective-permute-start | bytes 393224 | tf_op jit(solution)/shard_map/ppermute | solution.py:156
  236.6 43.7 %collective-permute-start.3 = (f32[2,2,256,1,32]{2,4,1,0,3:T(8,128)S(1)}, f32[2,2,256,1,32]{2,4,1,0,3:T(8,128)S(1)}, u32[]{:S(2)}, u32[]{:S(2)}) collective-permute-start(f32[2,2,256,1,32]{2,4,1,0,3:T(8,128)S(1)} %get-tuple-element.43), channel_id=1, source_target_pairs={{0,8},{2,10},{4,12},{6,14},{8,16},{10,18},{12,20},{14,22},{16,24},... | collective-permute-start | bytes 393224 | tf_op jit(solution)/shard_map/ppermute | solution.py:156
  238.1 59.6 %collective-permute-start.4 = (f32[2,2,256,1,32]{2,4,1,0,3:T(8,128)S(1)}, f32[2,2,256,1,32]{2,4,1,0,3:T(8,128)}, u32[]{:S(2)}, u32[]{:S(2)}) collective-permute-start(f32[2,2,256,1,32]{2,4,1,0,3:T(8,128)S(1)} %get-tuple-element.42), channel_id=1, source_target_pairs={{0,10},{2,12},{4,14},{6,16},{8,18},{10,20},{12,22},{14,24},{16,26}... | collective-permute-start | bytes 393224 | tf_op jit(solution)/shard_map/ppermute | solution.py:156
  264.2 38.1 %collective-permute-start.5 = (f32[2,2,256,1,32]{2,4,1,0,3:T(8,128)S(1)}, f32[2,2,256,1,32]{2,4,1,0,3:T(8,128)}, u32[]{:S(2)}, u32[]{:S(2)}) collective-permute-start(f32[2,2,256,1,32]{2,4,1,0,3:T(8,128)S(1)} %get-tuple-element.41), channel_id=1, source_target_pairs={{0,12},{2,14},{4,16},{6,18},{8,20},{10,22},{12,24},{14,26},{16,28}... | collective-permute-start | bytes 393224 | tf_op jit(solution)/shard_map/ppermute | solution.py:156
  265.3 38.0 %collective-permute-start.6 = (f32[2,2,256,1,32]{2,4,1,0,3:T(8,128)S(1)}, f32[2,2,256,1,32]{2,4,1,0,3:T(8,128)}, u32[]{:S(2)}, u32[]{:S(2)}) collective-permute-start(f32[2,2,256,1,32]{2,4,1,0,3:T(8,128)S(1)} %get-tuple-element.40), channel_id=1, source_target_pairs={{0,14},{2,16},{4,18},{6,20},{8,22},{10,24},{12,26},{14,28},{16,30}... | collective-permute-start | bytes 393224 | tf_op jit(solution)/shard_map/ppermute | solution.py:156
  279.8 26.6 %collective-permute-start.7 = (f32[2,2,256,1,32]{2,4,1,0,3:T(8,128)S(1)}, f32[2,2,256,1,32]{2,4,1,0,3:T(8,128)S(1)}, u32[]{:S(2)}, u32[]{:S(2)}) collective-permute-start(f32[2,2,256,1,32]{2,4,1,0,3:T(8,128)S(1)} %get-tuple-element.39), channel_id=1, source_target_pairs={{0,16},{2,18},{4,20},{6,22},{8,24},{10,26},{12,28},{14,30},{16,0},... | collective-permute-start | bytes 393224 | tf_op jit(solution)/shard_map/ppermute | solution.py:156
  280.3 0.7 copy-start.7
  281.0 27.2 %collective-permute-start.8 = (f32[2,2,256,1,32]{2,4,1,0,3:T(8,128)S(1)}, f32[2,2,256,1,32]{2,4,1,0,3:T(8,128)S(1)}, u32[]{:S(2)}, u32[]{:S(2)}) collective-permute-start(f32[2,2,256,1,32]{2,4,1,0,3:T(8,128)S(1)} %get-tuple-element.38), channel_id=1, source_target_pairs={{0,18},{2,20},{4,22},{6,24},{8,26},{10,28},{12,30},{14,0},{16,2},{... | collective-permute-start | bytes 393224 | tf_op jit(solution)/shard_map/ppermute | solution.py:156
  283.3 112.2 %all-to-all-start.6 = ((f32[2,32,256,1,32]{2,4,0,3,1:T(8,128)}), f32[2,32,256,1,32]{2,4,0,3,1:T(8,128)}, u32[]{:S(2)}, u32[]{:S(2)}) async-start(f32[2,32,256,1,32]{2,4,0,3,1:T(8,128)} %copy.165), calls=%async_computation.7 | async-start | bytes 4194304 | tf_op jit(solution)/shard_map/all_to_all | solution.py:171
  297.7 38.9 %collective-permute-start.9 = (f32[2,2,256,1,32]{2,4,1,0,3:T(8,128)S(1)}, f32[2,2,256,1,32]{2,4,1,0,3:T(8,128)S(1)}, u32[]{:S(2)}, u32[]{:S(2)}) collective-permute-start(f32[2,2,256,1,32]{2,4,1,0,3:T(8,128)S(1)} %get-tuple-element.37), channel_id=1, source_target_pairs={{0,20},{2,22},{4,24},{6,26},{8,28},{10,30},{12,0},{14,2},{16,4},{1... | collective-permute-start | bytes 393224 | tf_op jit(solution)/shard_map/ppermute | solution.py:156
  302.3 96.8 %collective-permute-start.10 = (f32[2,2,256,1,32]{2,4,1,0,3:T(8,128)}, f32[2,2,256,1,32]{2,4,1,0,3:T(8,128)}, u32[]{:S(2)}, u32[]{:S(2)}) collective-permute-start(f32[2,2,256,1,32]{2,4,1,0,3:T(8,128)} %get-tuple-element.36), channel_id=1, source_target_pairs={{0,22},{2,24},{4,26},{6,28},{8,30},{10,0},{12,2},{14,4},{16,6},{18... | collective-permute-start | bytes 393224 | tf_op jit(solution)/shard_map/ppermute | solution.py:156
  303.3 96.8 %collective-permute-start.11 = (f32[2,2,256,1,32]{2,4,1,0,3:T(8,128)}, f32[2,2,256,1,32]{2,4,1,0,3:T(8,128)}, u32[]{:S(2)}, u32[]{:S(2)}) collective-permute-start(f32[2,2,256,1,32]{2,4,1,0,3:T(8,128)} %get-tuple-element.35), channel_id=1, source_target_pairs={{0,24},{2,26},{4,28},{6,30},{8,0},{10,2},{12,4},{14,6},{16,8},{18,... | collective-permute-start | bytes 393224 | tf_op jit(solution)/shard_map/ppermute | solution.py:156
  306.4 94.6 %collective-permute-start.12 = (f32[2,2,256,1,32]{2,4,1,0,3:T(8,128)}, f32[2,2,256,1,32]{2,4,1,0,3:T(8,128)}, u32[]{:S(2)}, u32[]{:S(2)}) collective-permute-start(f32[2,2,256,1,32]{2,4,1,0,3:T(8,128)} %get-tuple-element.34), channel_id=1, source_target_pairs={{0,26},{2,28},{4,30},{6,0},{8,2},{10,4},{12,6},{14,8},{16,10},{18,... | collective-permute-start | bytes 393224 | tf_op jit(solution)/shard_map/ppermute | solution.py:156
  308.2 93.7 %collective-permute-start.13 = (f32[2,2,256,1,32]{2,4,1,0,3:T(8,128)S(1)}, f32[2,2,256,1,32]{2,4,1,0,3:T(8,128)}, u32[]{:S(2)}, u32[]{:S(2)}) collective-permute-start(f32[2,2,256,1,32]{2,4,1,0,3:T(8,128)S(1)} %get-tuple-element.33), channel_id=1, source_target_pairs={{0,28},{2,30},{4,0},{6,2},{8,4},{10,6},{12,8},{14,10},{16,12},{18,... | collective-permute-start | bytes 393224 | tf_op jit(solution)/shard_map/ppermute | solution.py:156
  336.5 66.3 %collective-permute-start.14 = (f32[2,2,256,1,32]{2,4,1,0,3:T(8,128)S(1)}, f32[2,2,256,1,32]{2,4,1,0,3:T(8,128)}, u32[]{:S(2)}, u32[]{:S(2)}) collective-permute-start(f32[2,2,256,1,32]{2,4,1,0,3:T(8,128)S(1)} %get-tuple-element.32), channel_id=1, source_target_pairs={{0,30},{2,0},{4,2},{6,4},{8,6},{10,8},{12,10},{14,12},{16,14},{18,... | collective-permute-start | bytes 393224 | tf_op jit(solution)/shard_map/ppermute | solution.py:156
  395.6 28.9 %all-to-all-start.7 = ((bf16[16,2,8192]{2,1,0:T(2,128)(2,1)}), bf16[16,2,8192]{2,1,0:T(2,128)(2,1)S(1)}, u32[]{:S(2)}, u32[]{:S(2)}) async-start(bf16[16,2,8192]{2,1,0:T(2,128)(2,1)} %reshape.344), calls=%async_computation.8 | async-start | bytes 1048576 | tf_op jit(solution)/shard_map/all_to_all | solution.py:175
  403.8 1.3 copy-start
Sparse Core Ops, SparseCore 0:
  144.4 33.1 reduce-scatter.1
  227.9 58.0 all-gather.1
